TPU v7x, 512 devices: a whole 4x4x16 slice. The times are simulated.
512 devices in a mesh: vec: 64 (over y, z), row: 8 (over x, core).
Axes of the slice: x: 4, y: 4, z: 16, core: 2. Of those that a mesh axis runs over, the one named last changes fastest.
Arguments:
- vectors: bfloat16 [8, 4096, 1024], P('row', 'vec'), may hold values from -6 to 6
- rotation: bfloat16 [1024, 1024], P(None, 'vec'), may hold values from -0.1875 to 0.1875
- blocks: bfloat16 [256, 8, 128, 128], P('row'), may hold values from -0.125 to 0.125
- column_blocks: int32 [256, 8], P('row'), may hold values from -2 to 257, as said below
Outputs:
- filtered: bfloat16 [8, 4096, 1024], P('row', 'vec')
Inputs may be any that keep to these rules, and one draw needn't show every extreme that they name: `column_blocks`: block row r of partition p = r // 32 lists 8 distinct column blocks between p * 32 - 2 and p * 32 + 33; the first block row of every partition lists the lowest of these and the last one the highest; column blocks outside 0 to 255 stand for zeros.
All inputs are finite; a program needn't handle non-finite values.
Results may differ from a plain program's by a relative error of at most 0.006.
Values may be sent and summed in bfloat16 or wider, within the bound.
A program may use at most 64 MiB of HBM per device.

v0:
```python
import jax
import jax.numpy as jnp
from jax import lax
from jax.sharding import PartitionSpec as P

BS = 128
HB = 2
STEPS = 4
centre = 0.3
half_width = 1.2


def with_halo(block, sides, width):
    for axis, dim in sides:
        count = lax.axis_size(axis)
        forward = [(i, i + 1) for i in range(count - 1)]
        backward = [(target, source) for source, target in forward]
        low = lax.ppermute(
            lax.slice_in_dim(block, block.shape[dim] - width, None, axis=dim), axis, forward
        )
        high = lax.ppermute(lax.slice_in_dim(block, 0, width, axis=dim), axis, backward)
        block = jnp.concatenate([low, block, high], axis=dim)
    return block


def apply_matrix(operand, blocks, offsets):
    extended = with_halo(operand, (("row", 1),), HB * BS)
    stacked = extended.reshape(extended.shape[0], -1, BS)
    picked = stacked[:, offsets]
    product = jnp.einsum("rjab,krjb->kra", blocks, picked, preferred_element_type=jnp.float32)
    return product.reshape(extended.shape[0], -1)


def filter_panel(vec_panel, blocks, offsets):
    previous = vec_panel.astype(jnp.float32)
    current = (apply_matrix(vec_panel, blocks, offsets) - centre * previous) / half_width
    for turn_index in range(STEPS - 1):
        operand = current.astype(jnp.bfloat16)
        following = (
            2.0 * (apply_matrix(operand, blocks, offsets) - centre * current) / half_width
            - previous
        )
        previous = current
        current = following
    return current.astype(jnp.bfloat16)


def local(vectors, rotation, blocks, column_blocks):
    local_rows = vectors[0]
    offsets = column_blocks - (lax.axis_index("row") * column_blocks.shape[0] - HB)
    contract = (((0,), (1,)), ((), ()))
    vec_panel = lax.dot_general(
        rotation,
        lax.all_gather(local_rows, "vec", axis=0, tiled=True),
        contract,
        preferred_element_type=jnp.float32,
    ).astype(jnp.bfloat16)
    filtered = filter_panel(vec_panel, blocks, offsets)
    returned = lax.all_to_all(filtered, "vec", split_axis=1, concat_axis=0, tiled=True)
    return jnp.transpose(returned)[None]


def solution(mesh):
    placed = (P("row", "vec", None), P(None, "vec"), P("row", None, None, None), P("row", None))
    return jax.shard_map(
        local, mesh=mesh, in_specs=placed, out_specs=P("row", "vec", None), check_vma=False
    )
```

profile of v0, /device:TPU:1, one launch (start us, length us, event | category | flops | bytes accessed | tf_op | source)
XLA Modules:
  0.0 266.6 jit_solution(13129486595092253713)
XLA Ops:
  8.1 156.6 %all-gather.3.cloned.1.call-done = bf16[1,4096,1024]{2,1,0:T(8,128)(2,1)} async-done(((bf16[1,64,1024]{2,1,0:T(8,128)(2,1)}), bf16[1,4096,1024]{2,1,0:T(8,128)(2,1)}) %all-gather.3.cloned.1.call-update) | async-done | bytes 8388624 | tf_op jit(solution)/shard_map/all_gather | solution.py:54
  164.7 5.7 %fusion.2 = bf16[16,4096]{1,0:T(8,128)(2,1)S(1)} fusion(bf16[1024,16]{0,1:T(8,128)(2,1)S(1)} %copy-done, bf16[1,4096,1024]{2,1,0:T(8,128)(2,1)} %all-gather.3.cloned.1.call-done), kind=kOutput, calls=%fused_computation.6 | convolution fusion | flops 134283264 | bytes 8552448 | tf_op jit(solution)/shard_map/dot_general | solution.py:52
  170.4 11.5 %collective-permute-start = (bf16[16,256]{1,0:T(8,128)(2,1)S(1)}, bf16[16,256]{1,0:T(8,128)(2,1)S(1)}, u32[]{:S(2)}, u32[]{:S(2)}) collective-permute-start(bf16[16,256]{1,0:T(8,128)(2,1)S(1)} %get-tuple-element.11), channel_id=1, source_target_pairs={{0,1},{1,2},{2,3},{3,4},{4,5},{5,6},{6,7},{8,9},{9,10},{10,11},{11... | collective-permute-start | bytes 24584 | tf_op jit(solution)/shard_map/ppermute | solution.py:18
  181.8 1.9 collective-permute-start.1
  183.8 3.0 %collective-permute-done.1 = bf16[16,256]{1,0:T(8,128)(2,1)S(1)} collective-permute-done((bf16[16,256]{1,0:T(8,128)(2,1)S(1)}, bf16[16,256]{1,0:T(8,128)(2,1)S(1)}, u32[]{:S(2)}, u32[]{:S(2)}) %collective-permute-start.1) | collective-permute-done | bytes 8224 | tf_op jit(solution)/shard_map/ppermute | solution.py:21
  186.8 0.8 gather_fusion
  187.7 5.7 %convolution_bitcast_fusion.3 = f32[32,2,8,128]{3,2,1,0:T(8,128)S(1)} fusion(bf16[16,32,8,128]{3,0,2,1:T(8,128)(2,1)S(1)} %bitcast.130, bf16[32,8,128,128]{3,2,1,0:T(8,128)(2,1)} %param.6), kind=kOutput, calls=%fused_computation.10 | convolution fusion | flops 134217728 | bytes 9699328 | tf_op jit(solution)/shard_map/rjab,krjb->kra/dot_general | solution.py:30
  193.4 1.9 collective-permute-start.2
  195.4 2.4 collective-permute-start.3
  197.8 2.6 collective-permute-done.3
  200.4 0.8 gather_fusion.1
  201.2 5.7 %convolution_bitcast_fusion.2 = f32[32,2,8,128]{3,2,1,0:T(8,128)S(1)} fusion(bf16[16,32,8,128]{3,0,2,1:T(8,128)(2,1)S(1)} %bitcast.131, bf16[32,8,128,128]{3,2,1,0:T(8,128)(2,1)} %param.6), kind=kOutput, calls=%fused_computation.9 | convolution fusion | flops 134217728 | bytes 9699328 | tf_op jit(solution)/shard_map/rjab,krjb->kra/dot_general | solution.py:30
  207.0 1.9 collective-permute-start.4
  209.0 2.4 collective-permute-start.5
  211.4 2.6 collective-permute-done.5
  214.0 0.8 gather_fusion.2
  214.8 5.7 %convolution_bitcast_fusion.1 = f32[32,2,8,128]{3,2,1,0:T(8,128)S(1)} fusion(bf16[16,32,8,128]{3,0,2,1:T(8,128)(2,1)S(1)} %bitcast.132, bf16[32,8,128,128]{3,2,1,0:T(8,128)(2,1)} %param.6), kind=kOutput, calls=%fused_computation.8 | convolution fusion | flops 134217728 | bytes 9699328 | tf_op jit(solution)/shard_map/rjab,krjb->kra/dot_general | solution.py:30
  220.6 1.9 collective-permute-start.6
  222.6 2.4 collective-permute-start.7
  225.0 2.6 collective-permute-done.7
  227.6 0.8 gather_fusion.3
  228.4 5.7 %convolution_bitcast_fusion = f32[32,2,8,128]{3,2,1,0:T(8,128)S(1)} fusion(bf16[16,32,8,128]{3,0,2,1:T(8,128)(2,1)S(1)} %bitcast.129, bf16[32,8,128,128]{3,2,1,0:T(8,128)(2,1)} %param.6), kind=kOutput, calls=%fused_computation.7 | convolution fusion | flops 134217728 | bytes 9699328 | tf_op jit(solution)/shard_map/rjab,krjb->kra/dot_general | solution.py:30
  234.9 23.9 %all_to_all.19 = bf16[64,2,512]{2,1,0:T(2,128)(2,1)S(1)} all-to-all(bf16[64,2,512]{2,1,0:T(2,128)(2,1)S(1)} %reshape.80), channel_id=1, replica_groups=mesh['vec'=64,'row'=8] {'vec'}, dimensions={0} | all-to-all | bytes 262144 | tf_op jit(solution)/shard_map/all_to_all | solution.py:59
  259.0 0.8 copy.24
  (28 shorter events, 3.0 us)
Async XLA Ops:
  6.5 158.2 %copy-start = (bf16[1024,16]{0,1:T(8,128)(2,1)S(1)}, bf16[1024,16]{0,1:T(8,128)(2,1)}, u32[]{:S(2)}) copy-start(bf16[1024,16]{0,1:T(8,128)(2,1)} %param.5) | copy-start | bytes 98308
  6.5 158.2 %all-gather.3.cloned.1.call-start = ((), (), s32[]{:S(2)}) async-start(), calls=%async_computation.1 | async-start | bytes 8519680 | tf_op jit(solution)/shard_map/all_gather | solution.py:54
  170.4 13.4 %collective-permute-start = (bf16[16,256]{1,0:T(8,128)(2,1)S(1)}, bf16[16,256]{1,0:T(8,128)(2,1)S(1)}, u32[]{:S(2)}, u32[]{:S(2)}) collective-permute-start(bf16[16,256]{1,0:T(8,128)(2,1)S(1)} %get-tuple-element.11), channel_id=1, source_target_pairs={{0,1},{1,2},{2,3},{3,4},{4,5},{5,6},{6,7},{8,9},{9,10},{10,11},{11... | collective-permute-start | bytes 24584 | tf_op jit(solution)/shard_map/ppermute | solution.py:18
  181.8 5.0 %collective-permute-start.1 = (bf16[16,256]{1,0:T(8,128)(2,1)S(1)}, bf16[16,256]{1,0:T(8,128)(2,1)S(1)}, u32[]{:S(2)}, u32[]{:S(2)}) collective-permute-start(bf16[16,256]{1,0:T(8,128)(2,1)S(1)} %get-tuple-element.12), channel_id=1, source_target_pairs={{1,0},{2,1},{3,2},{4,3},{5,4},{6,5},{7,6},{9,8},{10,9},{11,10},{12... | collective-permute-start | bytes 24584 | tf_op jit(solution)/shard_map/ppermute | solution.py:21
  193.4 4.3 %collective-permute-start.2 = (bf16[16,256]{1,0:T(8,128)(2,1)S(1)}, bf16[16,256]{1,0:T(8,128)(2,1)S(1)}, u32[]{:S(2)}, u32[]{:S(2)}) collective-permute-start(bf16[16,256]{1,0:T(8,128)(2,1)S(1)} %get-tuple-element.9), channel_id=1, source_target_pairs={{0,1},{1,2},{2,3},{3,4},{4,5},{5,6},{6,7},{8,9},{9,10},{10,11},{11... | collective-permute-start | bytes 24584 | tf_op jit(solution)/shard_map/ppermute | solution.py:18
  195.4 5.0 %collective-permute-start.3 = (bf16[16,256]{1,0:T(8,128)(2,1)S(1)}, bf16[16,256]{1,0:T(8,128)(2,1)S(1)}, u32[]{:S(2)}, u32[]{:S(2)}) collective-permute-start(bf16[16,256]{1,0:T(8,128)(2,1)S(1)} %get-tuple-element.10), channel_id=1, source_target_pairs={{1,0},{2,1},{3,2},{4,3},{5,4},{6,5},{7,6},{9,8},{10,9},{11,10},{12... | collective-permute-start | bytes 24584 | tf_op jit(solution)/shard_map/ppermute | solution.py:21
  207.0 4.3 %collective-permute-start.4 = (bf16[16,256]{1,0:T(8,128)(2,1)S(1)}, bf16[16,256]{1,0:T(8,128)(2,1)S(1)}, u32[]{:S(2)}, u32[]{:S(2)}) collective-permute-start(bf16[16,256]{1,0:T(8,128)(2,1)S(1)} %get-tuple-element.7), channel_id=1, source_target_pairs={{0,1},{1,2},{2,3},{3,4},{4,5},{5,6},{6,7},{8,9},{9,10},{10,11},{11... | collective-permute-start | bytes 24584 | tf_op jit(solution)/shard_map/ppermute | solution.py:18
  209.0 5.0 %collective-permute-start.5 = (bf16[16,256]{1,0:T(8,128)(2,1)S(1)}, bf16[16,256]{1,0:T(8,128)(2,1)S(1)}, u32[]{:S(2)}, u32[]{:S(2)}) collective-permute-start(bf16[16,256]{1,0:T(8,128)(2,1)S(1)} %get-tuple-element.8), channel_id=1, source_target_pairs={{1,0},{2,1},{3,2},{4,3},{5,4},{6,5},{7,6},{9,8},{10,9},{11,10},{12... | collective-permute-start | bytes 24584 | tf_op jit(solution)/shard_map/ppermute | solution.py:21
  220.6 4.3 %collective-permute-start.6 = (bf16[16,256]{1,0:T(8,128)(2,1)S(1)}, bf16[16,256]{1,0:T(8,128)(2,1)S(1)}, u32[]{:S(2)}, u32[]{:S(2)}) collective-permute-start(bf16[16,256]{1,0:T(8,128)(2,1)S(1)} %get-tuple-element.5), channel_id=1, source_target_pairs={{0,1},{1,2},{2,3},{3,4},{4,5},{5,6},{6,7},{8,9},{9,10},{10,11},{11... | collective-permute-start | bytes 24584 | tf_op jit(solution)/shard_map/ppermute | solution.py:18
  222.6 5.0 %collective-permute-start.7 = (bf16[16,256]{1,0:T(8,128)(2,1)S(1)}, bf16[16,256]{1,0:T(8,128)(2,1)S(1)}, u32[]{:S(2)}, u32[]{:S(2)}) collective-permute-start(bf16[16,256]{1,0:T(8,128)(2,1)S(1)} %get-tuple-element.6), channel_id=1, source_target_pairs={{1,0},{2,1},{3,2},{4,3},{5,4},{6,5},{7,6},{9,8},{10,9},{11,10},{12... | collective-permute-start | bytes 24584 | tf_op jit(solution)/shard_map/ppermute | solution.py:21
Sparse Core Ops, SparseCore 0:
  10.3 154.3 all-gather.2
where the time goes:
time: 267 us
  waiting for transfers between devices  168 us (63%)
  matrix products  28.3 us (11%)
  starting transfers between devices  26.3 us (10%)
  blocking collectives  23.9 us (9%)
  between operations  13.6 us (5%)
  local copies, waits for them, and re-layouts  5.19 us (2%)
    all_gather x1, waiting for transfers between devices, local(): lax.all_gather(local_rows, 'vec', axis=0, tiled=True)  157 us
    all_to_all x1, blocking collectives, local(): lax.all_to_all(filtered, 'vec', split_axis=1, concat_axis=0, tiled=True)  23.9 us
    dot_general x4, matrix products, apply_matrix(): jnp.einsum('rjab,krjb->kra', blocks, picked, preferred_element_type=jnp.f...  22.6 us
    ppermute x4, starting transfers between devices, with_halo(): lax.ppermute(lax.slice_in_dim(block, block.shape[dim] - width, None, axis...  17.3 us
    ppermute x4, waiting for transfers between devices, with_halo(): lax.ppermute(lax.slice_in_dim(block, 0, width, axis=dim), axis, backward)  10.7 us
    ppermute x4, starting transfers between devices, with_halo(): lax.ppermute(lax.slice_in_dim(block, 0, width, axis=dim), axis, backward)  9.05 us
    dot_general x1, matrix products, local(): lax.dot_general(rotation, lax.all_gather(local_rows, 'vec', axis=0, tiled...  5.65 us
  transfers between devices with their start and end apart: 9, of which 5 were waited for; matrix products, arithmetic and copies ran while one was open for 0% of the time, Pallas kernels for 0%

commit v1 on v0

--- a/solution.py
+++ b/solution.py
@@ -8,6 +8,12 @@
 STEPS = 4
 centre = 0.3
 half_width = 1.2
+
+
+def threads_set(arr_in, across):
+    return jnp.concatenate(
+        lax.all_to_all(jnp.stack([arr_in] * lax.axis_size(across)), across, 0, 0), axis=0
+    )
 
 
 def with_halo(block, sides, width):
@@ -50,10 +56,7 @@
     offsets = column_blocks - (lax.axis_index("row") * column_blocks.shape[0] - HB)
     contract = (((0,), (1,)), ((), ()))
     vec_panel = lax.dot_general(
-        rotation,
-        lax.all_gather(local_rows, "vec", axis=0, tiled=True),
-        contract,
-        preferred_element_type=jnp.float32,
+        rotation, threads_set(local_rows, "vec"), contract, preferred_element_type=jnp.float32
     ).astype(jnp.bfloat16)
     filtered = filter_panel(vec_panel, blocks, offsets)
     returned = lax.all_to_all(filtered, "vec", split_axis=1, concat_axis=0, tiled=True)

time: 267 us -> 479 us (1.79)
  waiting for transfers between devices: 168 us -> 376 us
  starting transfers between devices: 26.3 us -> 40.4 us
  between operations: 13.6 us -> 0.25 us
  local copies, waits for them, and re-layouts: 5.19 us -> 10.4 us
    all_to_all x0 -> x1, waiting for transfers between devices: none -> 366 us  [threads_set(): lax.all_to_all(jnp.stack([arr_in] * lax.axis_size(across)), across, 0, 0)]
    all_gather x1 -> x0, waiting for transfers between devices: 157 us -> none  [local(): lax.all_gather(local_rows, 'vec', axis=0, tiled=True)]
    all_to_all x0 -> x1, starting transfers between devices: none -> 19.7 us  [threads_set(): lax.all_to_all(jnp.stack([arr_in] * lax.axis_size(across)), across, 0, 0)]
    ppermute x4, starting transfers between devices: 17.3 us -> 11.7 us  [with_halo(): lax.ppermute(lax.slice_in_dim(block, block.shape[dim] - width, None, axis...]
    another operation x0 -> x1, local copies, waits for them, and re-layouts: none -> 5.22 us  [threads_set(): jnp.stack([arr_in] * lax.axis_size(across))]
where the time goes in v1:
time: 479 us; the launch traced here: 478 us
  waiting for transfers between devices  376 us (78%)
  starting transfers between devices  40.4 us (8%)
  matrix products  28.3 us (6%)
  blocking collectives  22.1 us (5%)
  local copies, waits for them, and re-layouts  10.4 us (2%)
    all_to_all x1, waiting for transfers between devices, threads_set(): lax.all_to_all(jnp.stack([arr_in] * lax.axis_size(across)), across, 0, 0)  366 us
    dot_general x4, matrix products, apply_matrix(): jnp.einsum('rjab,krjb->kra', blocks, picked, preferred_element_type=jnp.f...  22.6 us
    all_to_all x1, blocking collectives, local(): lax.all_to_all(filtered, 'vec', split_axis=1, concat_axis=0, tiled=True)  22.1 us
    all_to_all x1, starting transfers between devices, threads_set(): lax.all_to_all(jnp.stack([arr_in] * lax.axis_size(across)), across, 0, 0)  19.7 us
    ppermute x4, starting transfers between devices, with_halo(): lax.ppermute(lax.slice_in_dim(block, block.shape[dim] - width, None, axis...  11.7 us
    ppermute x4, waiting for transfers between devices, with_halo(): lax.ppermute(lax.slice_in_dim(block, 0, width, axis=dim), axis, backward)  10.7 us
  transfers between devices with their start and end apart: 9, of which 5 were waited for; matrix products, arithmetic and copies ran while one was open for 0% of the time, Pallas kernels for 0%

profile of v1, /device:TPU:1, one launch (start us, length us, event | category | flops | bytes accessed | tf_op | source)
XLA Modules:
  0.0 478.5 jit_solution(16152196805968019871)
XLA Ops:
  0.0 5.2 %stack.3 = bf16[64,64,1024]{2,1,0:T(8,128)(2,1)} broadcast(bf16[64,1024]{1,0:T(8,128)(2,1)} %bitcast.133), dimensions={1,2} | broadcast | bytes 8519680 | tf_op jit(solution)/shard_map/stack | solution.py:15
  5.2 19.7 %all-to-all-start = ((bf16[64,64,1024]{2,1,0:T(8,128)(2,1)}), bf16[64,64,1024]{2,1,0:T(8,128)(2,1)}, u32[]{:S(2)}, u32[]{:S(2)}) async-start(bf16[64,64,1024]{2,1,0:T(8,128)(2,1)} %stack.3), calls=%async_computation | async-start | bytes 16777216 | tf_op jit(solution)/shard_map/all_to_all | solution.py:15
  25.1 365.7 %all-to-all-done = bf16[64,64,1024]{2,1,0:T(8,128)(2,1)} async-done(((bf16[64,64,1024]{2,1,0:T(8,128)(2,1)}), bf16[64,64,1024]{2,1,0:T(8,128)(2,1)}, u32[]{:S(2)}, u32[]{:S(2)}) %all-to-all-start) | async-done | bytes 8388640 | tf_op jit(solution)/shard_map/all_to_all | solution.py:15
  390.8 5.7 %convolution_convert_fusion = bf16[16,4096]{1,0:T(8,128)(2,1)S(1)} fusion(bf16[1024,16]{0,1:T(8,128)(2,1)S(1)} %copy-done, bf16[4096,1024]{1,0:T(8,128)(2,1)} %bitcast.1), kind=kOutput, calls=%fused_computation.4 | convolution fusion | flops 134283264 | bytes 8552448 | tf_op jit(solution)/shard_map/dot_general | solution.py:58
  396.4 5.8 %collective-permute-start = (bf16[16,256]{1,0:T(8,128)(2,1)S(1)}, bf16[16,256]{1,0:T(8,128)(2,1)S(1)}, u32[]{:S(2)}, u32[]{:S(2)}) collective-permute-start(bf16[16,256]{1,0:T(8,128)(2,1)S(1)} %get-tuple-element.11), channel_id=1, source_target_pairs={{0,1},{1,2},{2,3},{3,4},{4,5},{5,6},{6,7},{8,9},{9,10},{10,11},{11... | collective-permute-start | bytes 24584 | tf_op jit(solution)/shard_map/ppermute | solution.py:24
  402.3 1.9 collective-permute-start.1
  404.2 3.0 collective-permute-done.1
  407.3 0.8 gather_fusion
  408.1 5.7 %convolution_bitcast_fusion.3 = f32[32,2,8,128]{3,2,1,0:T(8,128)S(1)} fusion(bf16[16,32,8,128]{3,0,2,1:T(8,128)(2,1)S(1)} %bitcast.128, bf16[32,8,128,128]{3,2,1,0:T(8,128)(2,1)} %param.6), kind=kOutput, calls=%fused_computation.8 | convolution fusion | flops 134217728 | bytes 9699328 | tf_op jit(solution)/shard_map/rjab,krjb->kra/dot_general | solution.py:36
  413.9 1.9 collective-permute-start.2
  415.8 2.4 collective-permute-start.3
  418.2 2.6 collective-permute-done.3
  420.8 0.8 gather_fusion.1
  421.7 5.7 %convolution_bitcast_fusion.2 = f32[32,2,8,128]{3,2,1,0:T(8,128)S(1)} fusion(bf16[16,32,8,128]{3,0,2,1:T(8,128)(2,1)S(1)} %bitcast.129, bf16[32,8,128,128]{3,2,1,0:T(8,128)(2,1)} %param.6), kind=kOutput, calls=%fused_computation.7 | convolution fusion | flops 134217728 | bytes 9699328 | tf_op jit(solution)/shard_map/rjab,krjb->kra/dot_general | solution.py:36
  427.4 1.9 collective-permute-start.4
  429.4 2.4 collective-permute-start.5
  431.8 2.6 collective-permute-done.5
  434.4 0.8 gather_fusion.2
  435.2 5.7 %convolution_bitcast_fusion.1 = f32[32,2,8,128]{3,2,1,0:T(8,128)S(1)} fusion(bf16[16,32,8,128]{3,0,2,1:T(8,128)(2,1)S(1)} %bitcast.130, bf16[32,8,128,128]{3,2,1,0:T(8,128)(2,1)} %param.6), kind=kOutput, calls=%fused_computation.6 | convolution fusion | flops 134217728 | bytes 9699328 | tf_op jit(solution)/shard_map/rjab,krjb->kra/dot_general | solution.py:36
  441.0 1.9 collective-permute-start.6
  443.0 2.4 collective-permute-start.7
  445.4 2.6 collective-permute-done.7
  448.8 5.7 %convolution_bitcast_fusion = f32[32,2,8,128]{3,2,1,0:T(8,128)S(1)} fusion(bf16[16,32,8,128]{3,0,2,1:T(8,128)(2,1)S(1)} %bitcast.127, bf16[32,8,128,128]{3,2,1,0:T(8,128)(2,1)} %param.6), kind=kOutput, calls=%fused_computation.5 | convolution fusion | flops 134217728 | bytes 9699328 | tf_op jit(solution)/shard_map/rjab,krjb->kra/dot_general | solution.py:36
  455.3 22.1 %all_to_all.24 = bf16[64,2,512]{2,1,0:T(2,128)(2,1)S(1)} all-to-all(bf16[64,2,512]{2,1,0:T(2,128)(2,1)S(1)} %reshape.84), channel_id=1, replica_groups=mesh['vec'=64,'row'=8] {'vec'}, dimensions={0} | all-to-all | bytes 262144 | tf_op jit(solution)/shard_map/all_to_all | solution.py:62
  (30 shorter events, 3.2 us)
Async XLA Ops:
  0.0 390.8 %copy-start = (bf16[1024,16]{0,1:T(8,128)(2,1)S(1)}, bf16[1024,16]{0,1:T(8,128)(2,1)}, u32[]{:S(2)}) copy-start(bf16[1024,16]{0,1:T(8,128)(2,1)} %param.5) | copy-start | bytes 98308
  5.2 19.7 %copy-start.1 = (s32[32,8]{0,1:T(8,128)S(1)}, s32[32,8]{0,1:T(8,128)}, u32[]{:S(2)}) copy-start(s32[32,8]{0,1:T(8,128)} %param.7) | copy-start | bytes 3076
  5.2 385.5 %all-to-all-start = ((bf16[64,64,1024]{2,1,0:T(8,128)(2,1)}), bf16[64,64,1024]{2,1,0:T(8,128)(2,1)}, u32[]{:S(2)}, u32[]{:S(2)}) async-start(bf16[64,64,1024]{2,1,0:T(8,128)(2,1)} %stack.3), calls=%async_computation | async-start | bytes 16777216 | tf_op jit(solution)/shard_map/all_to_all | solution.py:15
  396.4 7.8 %collective-permute-start = (bf16[16,256]{1,0:T(8,128)(2,1)S(1)}, bf16[16,256]{1,0:T(8,128)(2,1)S(1)}, u32[]{:S(2)}, u32[]{:S(2)}) collective-permute-start(bf16[16,256]{1,0:T(8,128)(2,1)S(1)} %get-tuple-element.11), channel_id=1, source_target_pairs={{0,1},{1,2},{2,3},{3,4},{4,5},{5,6},{6,7},{8,9},{9,10},{10,11},{11... | collective-permute-start | bytes 24584 | tf_op jit(solution)/shard_map/ppermute | solution.py:24
  402.3 5.0 %collective-permute-start.1 = (bf16[16,256]{1,0:T(8,128)(2,1)S(1)}, bf16[16,256]{1,0:T(8,128)(2,1)S(1)}, u32[]{:S(2)}, u32[]{:S(2)}) collective-permute-start(bf16[16,256]{1,0:T(8,128)(2,1)S(1)} %get-tuple-element.12), channel_id=1, source_target_pairs={{1,0},{2,1},{3,2},{4,3},{5,4},{6,5},{7,6},{9,8},{10,9},{11,10},{12... | collective-permute-start | bytes 24584 | tf_op jit(solution)/shard_map/ppermute | solution.py:27
  413.9 4.3 collective-permute-start.2
  415.8 5.0 %collective-permute-start.3 = (bf16[16,256]{1,0:T(8,128)(2,1)S(1)}, bf16[16,256]{1,0:T(8,128)(2,1)S(1)}, u32[]{:S(2)}, u32[]{:S(2)}) collective-permute-start(bf16[16,256]{1,0:T(8,128)(2,1)S(1)} %get-tuple-element.10), channel_id=1, source_target_pairs={{1,0},{2,1},{3,2},{4,3},{5,4},{6,5},{7,6},{9,8},{10,9},{11,10},{12... | collective-permute-start | bytes 24584 | tf_op jit(solution)/shard_map/ppermute | solution.py:27
  427.4 4.3 collective-permute-start.4
  429.4 5.0 %collective-permute-start.5 = (bf16[16,256]{1,0:T(8,128)(2,1)S(1)}, bf16[16,256]{1,0:T(8,128)(2,1)S(1)}, u32[]{:S(2)}, u32[]{:S(2)}) collective-permute-start(bf16[16,256]{1,0:T(8,128)(2,1)S(1)} %get-tuple-element.8), channel_id=1, source_target_pairs={{1,0},{2,1},{3,2},{4,3},{5,4},{6,5},{7,6},{9,8},{10,9},{11,10},{12... | collective-permute-start | bytes 24584 | tf_op jit(solution)/shard_map/ppermute | solution.py:27
  441.0 4.3 collective-permute-start.6
  443.0 5.0 %collective-permute-start.7 = (bf16[16,256]{1,0:T(8,128)(2,1)S(1)}, bf16[16,256]{1,0:T(8,128)(2,1)S(1)}, u32[]{:S(2)}, u32[]{:S(2)}) collective-permute-start(bf16[16,256]{1,0:T(8,128)(2,1)S(1)} %get-tuple-element.6), channel_id=1, source_target_pairs={{1,0},{2,1},{3,2},{4,3},{5,4},{6,5},{7,6},{9,8},{10,9},{11,10},{12... | collective-permute-start | bytes 24584 | tf_op jit(solution)/shard_map/ppermute | solution.py:27
